TPU v7x, 256 devices: a whole 4x4x8 slice. The times are simulated.
256 devices in a mesh: pop: 32 (over x, y, core), row: 8 (over z).
Axes of the slice: x: 4, y: 4, z: 8, core: 2. Of those that a mesh axis runs over, the one named last changes fastest.
Arguments:
- tokens: bfloat16 [1536, 16, 4096], P('pop'), may hold values from -6 to 6
- weight: bfloat16 [14336, 4096], P('row', 'pop'), may hold values from -0.09375 to 0.09375
- bank_in: bfloat16 [4096, 128], P('row'), may hold values from -0.09375 to 0.09375
- bank_out: bfloat16 [14336, 128], P('row'), may hold values from -6 to 6
- fitness: int32 [1536], P('pop'), may hold values from 0 to 767
- past_seeds: int32 [1536, 2, 8], P('pop'), may hold values from 0 to 127
- new_seeds: int32 [1536, 2, 8], P('pop'), may hold values from 0 to 127
Outputs:
- hidden: bfloat16 [1536, 16, 14336], P('pop', None, 'row')
- new_weight: bfloat16 [14336, 4096], P('row', 'pop')
All inputs are finite; a program needn't handle non-finite values.
Results may differ from a plain program's by a relative error of at most 0.012.
Values may be sent and summed in bfloat16 or wider, within the bound.
A program may use at most 128 MiB of HBM per device.

v0:
```python
import jax
import jax.numpy as jnp
from jax import lax
from jax.sharding import Mesh
from jax.sharding import PartitionSpec as P

POP = ("pop_0", "pop_1", "pop_2")


NOISE_SCALE = 0.1
STEP_SCALE = 0.03


def sent_to_all(array, axis):
    count = lax.axis_size(axis)
    return lax.all_to_all(
        jnp.broadcast_to(array[None], (count, *array.shape)), axis, 0, 0, tiled=True
    )


def laid_out(blocks, dim):
    shape = list(blocks.shape[1:])
    shape[dim] *= blocks.shape[0]
    return jnp.moveaxis(blocks, 0, dim).reshape(shape)


def gather_directly(array, axis, dim):
    blocks = sent_to_all(array, axis)
    return laid_out(blocks, dim)


def filled_up(lines, count):
    spare = -len(lines) % count
    return jnp.pad(lines, [(0, spare)] + [(0, 0)] * (lines.ndim - 1))


def own_block(blocks, axes, sequence):
    shape = [lax.axis_size(a) for a in axes]
    blocks = blocks.reshape(*shape, *blocks.shape[1:])
    blocks = blocks.transpose(*sequence, *range(len(axes), blocks.ndim))
    blocks = blocks.reshape(-1, *blocks.shape[len(axes) :])
    for k in sequence:
        blocks = lax.psum_scatter(blocks, axes[k], scatter_dimension=0, tiled=True)
    return blocks[0]


def all_blocks(array, axes, sequence):
    blocks = array[None]
    for k in sequence:
        blocks = lax.all_gather(blocks, axes[k], axis=0, tiled=True)
    block = [lax.axis_size(axes[k]) for k in reversed(sequence)]
    blocks = blocks.reshape(*block, *array.shape)
    turned = sorted(range(len(sequence)), key=lambda place: sequence[len(sequence) - 1 - place])
    return blocks.transpose(*turned, *range(len(sequence), blocks.ndim)).reshape(-1, *array.shape)


def sum_by_parts(array, axes, sequence):
    count, lines = (lax.axis_size(axes), array.reshape(-1, *array.shape[1:][-1:]))
    blocks = filled_up(lines, count).reshape(count, -1, *lines.shape[1:])
    own = own_block(blocks, axes, sequence)
    whole = all_blocks(own, axes, sequence[::-1]).reshape(-1, *lines.shape[1:])
    return whole[: len(lines)].reshape(array.shape)


def one_hots(seeds, width):
    levels = jnp.arange(width, dtype=jnp.int32)
    out_hits = (seeds[:, 0, :, None] == levels).astype(jnp.float32)
    in_hits = (seeds[:, 1, :, None] == levels).astype(jnp.float32)
    return (out_hits, in_hits)


def shards(tokens, weight, bank_in, bank_out, fitness, past_seeds, new_seeds):
    members = fitness.shape[0]
    overall = members * lax.axis_size(POP)
    width = bank_out.shape[1]
    everyone = gather_directly(fitness, POP, 0)
    lower_count = jnp.sum((everyone[None, :] < fitness[:, None]).astype(jnp.float32), axis=1)
    equal_count = jnp.sum((everyone[None, :] == fitness[:, None]).astype(jnp.float32), axis=1)
    centered = (lower_count + 0.5 * (equal_count - 1.0)) / (overall - 1.0) - 0.5
    out_hits, in_hits = one_hots(past_seeds, width)
    local_coupling = STEP_SCALE * jnp.einsum("m,mki,mkj->ij", centered, out_hits, in_hits)
    coupling = sum_by_parts(local_coupling, POP, (1, 2, 0))
    full_in = gather_directly(bank_in, "row", 0)
    left_part = jnp.dot(bank_out.astype(jnp.float32), coupling)

    def refresh(portion, offset):
        columns = lax.dynamic_slice_in_dim(full_in, offset, portion.shape[1], 0).astype(jnp.float32)
        update = jnp.dot(left_part, columns.T)
        return (portion.astype(jnp.float32) + update).astype(jnp.bfloat16)

    features = tokens.shape[2]
    flat_tokens = tokens.reshape(members * tokens.shape[1], features)
    own_offset = lax.axis_index(POP) * weight.shape[1]
    new_weight = refresh(weight, own_offset)
    columns = flat_tokens
    base_part = lax.dot_general(
        columns,
        refresh(lax.all_gather(weight, POP, axis=1, tiled=True), jnp.int32(0)),
        (((1,), (1,)), ((), ())),
        preferred_element_type=jnp.float32,
    )
    projected = jnp.dot(flat_tokens, full_in, preferred_element_type=jnp.float32).reshape(
        members, tokens.shape[1], width
    )
    hidden_hits, feature_hits = one_hots(new_seeds, width)
    mixing = jnp.einsum("mkb,mkc->mbc", feature_hits, hidden_hits)
    low_term = (NOISE_SCALE * jnp.einsum("mtb,mbc->mtc", projected, mixing)).astype(jnp.bfloat16)
    extra = lax.dot_general(
        low_term.reshape(flat_tokens.shape[0], width),
        bank_out,
        (((1,), (1,)), ((), ())),
        preferred_element_type=jnp.float32,
    )
    hidden = (
        (base_part + extra).astype(jnp.bfloat16).reshape(members, tokens.shape[1], weight.shape[0])
    )
    return (hidden, new_weight)


def solution(mesh):
    torus = Mesh(
        mesh.devices.reshape(4, 4, 2, mesh.shape["row"]), ("pop_0", "pop_1", "pop_2", "row")
    )
    return jax.shard_map(
        shards,
        mesh=torus,
        in_specs=(
            P(POP, None, None),
            P("row", POP),
            P("row", None),
            P("row", None),
            P(POP),
            P(POP, None, None),
            P(POP, None, None),
        ),
        out_specs=(P(POP, None, "row"), P("row", POP)),
        check_vma=False,
    )
```

profile of v0, /device:TPU:1, one launch (start us, length us, event | category | flops | bytes accessed | tf_op | source)
XLA Modules:
  0.0 146.2 jit_solution(3092818776538204667)
XLA Ops:
  8.0 0.0 copy-start
  8.0 1.3 broadcast_in_dim.4
  9.3 8.6 %all-to-all-start = ((s32[32,1,48]{2,1,0:T(1,128)}), s32[32,1,48]{2,1,0:T(1,128)S(1)}, u32[]{:S(2)}, u32[]{:S(2)}) async-start(s32[32,1,48]{2,1,0:T(1,128)} %broadcast_in_dim.4), calls=%async_computation | async-start | bytes 32768 | tf_op jit(solution)/shard_map/all_to_all | solution.py:16
  17.9 0.0 reduce-scatter.3.cloned.1.call-start
  18.0 0.7 slice_bitcast_fusion.3
  18.7 6.1 %all-to-all-done = s32[32,1,48]{2,1,0:T(1,128)S(1)} async-done(((s32[32,1,48]{2,1,0:T(1,128)}), s32[32,1,48]{2,1,0:T(1,128)S(1)}, u32[]{:S(2)}, u32[]{:S(2)}) %all-to-all-start) | async-done | bytes 6176 | tf_op jit(solution)/shard_map/all_to_all | solution.py:16
  24.8 0.5 broadcast.33
  25.3 0.7 reduce.3
  26.0 0.1 lt.18
  26.1 0.9 convert_reduce_fusion
  27.0 0.4 fusion.18
  27.4 0.7 copy.25
  28.1 0.0 reduce-scatter.3.cloned.1.call-update
  28.1 0.0 all-gather.2.cloned.1.call-start
  28.1 0.5 all-gather.2.cloned.1.call-update
  28.7 2.0 %broadcast_in_dim.5 = bf16[8,512,128]{2,1,0:T(8,128)(2,1)} broadcast(bf16[512,128]{1,0:T(8,128)(2,1)} %param.9), dimensions={1,2} | broadcast | bytes 1179648 | tf_op jit(solution)/shard_map/broadcast_in_dim | solution.py:17
  30.7 8.2 %all-to-all-start.1 = ((bf16[8,512,128]{2,1,0:T(8,128)(2,1)}), bf16[8,512,128]{2,1,0:T(8,128)(2,1)S(1)}, u32[]{:S(2)}, u32[]{:S(2)}) async-start(bf16[8,512,128]{2,1,0:T(8,128)(2,1)} %broadcast_in_dim.5), calls=%async_computation.2 | async-start | bytes 2097152 | tf_op jit(solution)/shard_map/all_to_all | solution.py:16
  38.9 1.3 dynamic-slice
  40.1 1.3 dynamic-slice.2
  41.5 0.7 slice_bitcast_fusion.1
  42.2 0.1 copy.29
  42.3 0.1 copy.28
  43.0 7.6 %reduce-scatter.3.cloned.1.call-done = f32[8,4,128]{2,0,1:T(8,128)} async-done(((f32[32,4,128]{2,0,1:T(8,128)}), f32[8,4,128]{2,0,1:T(8,128)}) %reduce-scatter.3.cloned.1.call-update) | async-done | bytes 16400 | tf_op jit(solution)/shard_map/reduce_scatter | solution.py:43
  50.6 5.0 %all-reduce = f32[8,4,128]{2,0,1:T(8,128)S(1)} all-reduce(f32[8,4,128]{2,0,1:T(8,128)} %reduce-scatter.3.cloned.1.call-done), channel_id=3, replica_groups=mesh['pop_0'=4,'pop_1'=4,'pop_2'=2,'row'=8] {'pop_2'}, use_global_device_ids=true, to_apply=%region_3.4.clone | all-reduce | flops 4096 | bytes 32768
  55.6 8.8 %all-reduce.1 = bf16[4,4,128]{2,1,0:T(4,128)(2,1)S(1)} all-reduce(f32[4,4,128]{2,1,0:T(4,128)S(1)} %copy.26), channel_id=4, replica_groups=mesh['pop_0'=4,'pop_1'=4,'pop_2'=2,'row'=8] {'pop_0'}, use_global_device_ids=true, to_apply=%region_4.5.clone | all-reduce | flops 2048 | bytes 12288
  64.4 0.7 constant_dynamic-slice_fusion
  65.2 5.3 %all_gather.13 = bf16[4,4,128]{2,1,0:T(4,128)(2,1)S(1)} all-gather(bf16[1,4,128]{2,1,0:T(4,128)(2,1)S(1)} %constant_dynamic-slice_fusion), channel_id=1, replica_groups=mesh['pop_0'=4,'pop_1'=4,'pop_2'=2,'row'=8] {'pop_0'}, dimensions={0}, use_global_device_ids=true | all-gather | bytes 5120 | tf_op jit(solution)/shard_map/all_gather | solution.py:50
  70.4 5.1 %all_gather.14 = bf16[8,4,128]{2,1,0:T(4,128)(2,1)S(1)} all-gather(bf16[4,4,128]{2,1,0:T(4,128)(2,1)S(1)} %all_gather.13), channel_id=1, replica_groups=mesh['pop_0'=4,'pop_1'=4,'pop_2'=2,'row'=8] {'pop_2'}, dimensions={0}, use_global_device_ids=true | all-gather | bytes 12288 | tf_op jit(solution)/shard_map/all_gather | solution.py:50
  75.5 10.3 %all_gather.15 = bf16[32,4,128]{2,1,0:T(4,128)(2,1)S(1)} all-gather(bf16[8,4,128]{2,1,0:T(4,128)(2,1)S(1)} %all_gather.14), channel_id=1, replica_groups=mesh['pop_0'=4,'pop_1'=4,'pop_2'=2,'row'=8] {'pop_1'}, dimensions={0}, use_global_device_ids=true | all-gather | bytes 40960 | tf_op jit(solution)/shard_map/all_gather | solution.py:50
  85.8 0.0 copy-done
  85.8 0.3 fusion.31
  86.2 0.0 all-to-all-done.1
  86.2 2.1 %fusion.2 = bf16[1792,128]{1,0:T(8,128)(2,1)} fusion(bf16[128,1792]{1,0:T(8,128)(2,1)S(1)} %fusion.31, bf16[1792,128]{1,0:T(8,128)(2,1)} %param.8, bf16[4096,128]{1,0:T(8,128)(2,1)S(1)} %bitcast.43, s32[]{:T(128)S(6)} %select_n.3), kind=kOutput, calls=%fused_computation.5 | convolution fusion | flops 59408384 | bytes 1409028 | tf_op jit(solution)/shard_map/dot_general | solution.py:88
  88.3 6.1 %fusion.13 = bf16[48,16,128]{2,1,0:T(8,128)(2,1)S(1)} fusion(bf16[48,16,4096]{2,1,0:T(8,128)(2,1)} %param.7, bf16[4096,128,1]{1,0,2:T(8,128)(2,1)S(1)} %bitcast.44, s32[48,8]{1,0:T(8,128)S(1)} %copy.29, s32[48,8]{1,0:T(8,128)S(1)} %copy.28), kind=kOutput, calls=%fused_computation.10 | convolution fusion | flops 843350016 | bytes 7539712 | tf_op jit(solution)/shard_map/mtb,mbc->mtc/dot_general | solution.py:107
  94.4 15.8 %all-gather.2.cloned.1.call-done = bf16[1792,4096]{1,0:T(8,128)(2,1)} async-done(((bf16[1792,128]{1,0:T(8,128)(2,1)}), bf16[1792,4096]{1,0:T(8,128)(2,1)}) %all-gather.2.cloned.1.call-update) | async-done | bytes 14680080 | tf_op jit(solution)/shard_map/all_gather | solution.py:98
  110.2 23.6 %fusion.1 = f32[1792,768]{0,1:T(8,128)} fusion(bf16[768,4096]{1,0:T(8,128)(2,1)} %bitcast.51, bf16[1792,4096]{1,0:T(8,128)(2,1)} %all-gather.2.cloned.1.call-done, bf16[128,1792]{1,0:T(8,128)(2,1)S(1)} %fusion.31, bf16[4096,128]{1,0:T(8,128)(2,1)S(1)} %bitcast.45), kind=kOutput, calls=%fused_computation.3 | convolution fusion | flops 13175357440 | bytes 27983872 | tf_op jit(solution)/shard_map/dot_general | solution.py:96
  133.8 5.0 %fusion = bf16[768,1792]{1,0:T(8,128)(2,1)} fusion(f32[1792,768]{0,1:T(8,128)} %fusion.1, bf16[768,128]{1,0:T(8,128)(2,1)S(1)} %bitcast.47, bf16[1792,128]{1,0:T(8,128)(2,1)S(1)} %copy-done), kind=kOutput, calls=%fused_computation.2 | convolution fusion | flops 355074048 | bytes 8912896 | tf_op jit(solution)/shard_map/dot_general | solution.py:108
  (4 shorter events, 0.0 us)
Async XLA Ops:
  8.0 77.8 %copy-start = (bf16[1792,128]{1,0:T(8,128)(2,1)S(1)}, bf16[1792,128]{1,0:T(8,128)(2,1)}, u32[]{:S(2)}) copy-start(bf16[1792,128]{1,0:T(8,128)(2,1)} %param.10) | copy-start | bytes 1376260
  9.3 15.5 %all-to-all-start = ((s32[32,1,48]{2,1,0:T(1,128)}), s32[32,1,48]{2,1,0:T(1,128)S(1)}, u32[]{:S(2)}, u32[]{:S(2)}) async-start(s32[32,1,48]{2,1,0:T(1,128)} %broadcast_in_dim.4), calls=%async_computation | async-start | bytes 32768 | tf_op jit(solution)/shard_map/all_to_all | solution.py:16
  17.9 32.7 %reduce-scatter.3.cloned.1.call-start = ((), (), s32[]{:S(2)}) async-start(), calls=%async_computation.4 | async-start | bytes 81920 | tf_op jit(solution)/shard_map/reduce_scatter | solution.py:43
  28.1 82.1 %all-gather.2.cloned.1.call-start = ((), (), s32[]{:S(2)}) async-start(), calls=%async_computation.3 | async-start | bytes 15138816 | tf_op jit(solution)/shard_map/all_gather | solution.py:98
  30.7 55.5 %all-to-all-start.1 = ((bf16[8,512,128]{2,1,0:T(8,128)(2,1)}), bf16[8,512,128]{2,1,0:T(8,128)(2,1)S(1)}, u32[]{:S(2)}, u32[]{:S(2)}) async-start(bf16[8,512,128]{2,1,0:T(8,128)(2,1)} %broadcast_in_dim.5), calls=%async_computation.2 | async-start | bytes 2097152 | tf_op jit(solution)/shard_map/all_to_all | solution.py:16
Sparse Core Ops, SparseCore 0:
  28.2 22.3 reduce-scatter.2
Sparse Core Ops, SparseCore 1:
  31.0 79.0 all-gather.1
where the time goes:
time: 147 us; the launch traced here: 146 us
  matrix products  37.5 us (26%)
  blocking collectives  34.4 us (23%)
  waiting for transfers between devices  30.1 us (20%)
  starting transfers between devices  16.8 us (11%)
  between operations  16.2 us (11%)
  local copies, waits for them, and re-layouts  9.53 us (6%)
  other arithmetic  1.58 us (1%)
    dot_general x1, matrix products, shards(): lax.dot_general(columns, refresh(lax.all_gather(weight, POP, axis=1, tile...  23.6 us
    all_gather x3, blocking collectives, all_blocks(): blocks = lax.all_gather(blocks, axes[k], axis=0, tiled=True)  20.7 us
    all_to_all x2, starting transfers between devices, sent_to_all(): lax.all_to_all(jnp.broadcast_to(array[None], (count, *array.shape)), axis...  16.8 us
    all_gather x1, waiting for transfers between devices, shards(): lax.all_gather(weight, POP, axis=1, tiled=True)  15.8 us
    unnamed x2, blocking collectives  13.8 us
    reduce_scatter x1, waiting for transfers between devices, own_block(): blocks = lax.psum_scatter(blocks, axes[k], scatter_dimension=0, tiled=True)  7.64 us
    all_to_all x2, waiting for transfers between devices, sent_to_all(): lax.all_to_all(jnp.broadcast_to(array[None], (count, *array.shape)), axis...  6.14 us
    dot_general x1, matrix products, shards(): jnp.einsum('mtb,mbc->mtc', projected, mixing)  6.09 us
  transfers between devices with their start and end apart: 4, of which 3 were waited for; matrix products, arithmetic and copies ran while one was open for 11% of the time, Pallas kernels for 0%

commit v1 on v0

v1 whole, which is shorter than its diff:
```python
import functools

import jax
import jax.numpy as jnp
from jax import lax
from jax.experimental import pallas as pl
from jax.experimental.pallas import tpu as pltpu
from jax.sharding import Mesh
from jax.sharding import PartitionSpec as P

POP = ("pop_0", "pop_1", "pop_2")
MESH = pl.DeviceIdType.MESH

NOISE_SCALE = 0.1
STEP_SCALE = 0.03

RING = 4
DEPTH = 8
FAR = 1 << 20
F32 = jnp.float32
BF16 = jnp.bfloat16


def nt(a, b):
    return lax.dot_general(a, b, (((1,), (1,)), ((), ())), preferred_element_type=F32)


def nn(a, b):
    return jnp.dot(a, b, preferred_element_type=F32)


def halves(a):
    high = a.astype(BF16)
    return high, (a - high.astype(F32)).astype(BF16)


def slot(da, db):
    return (da % RING) * RING + db % RING


def one_hot_row(levels, row):
    return levels == jnp.broadcast_to(row, levels.shape)


def kernel(
    tok_hbm, w_hbm, bi_hbm, bo_hbm, small_hbm, seeds_hbm, hidden_hbm, nw_hbm,
    tok, w, bi, bo, small, seeds, acc, out, nw, weights, coup, zz,
    send, recv, sib_send, sib_recv, z_send, z_recv, s_send, s_recv, tok_sem, local, done,
):
    x, y, c, z = (lax.axis_index(name) for name in (*POP, "row"))
    rows = w_hbm.shape[0]
    half = rows // 2
    mine = x, y
    other = 1 - c

    def place(da, db, color):
        px = (x + da * (1 - color) + db * color) % RING
        py = (y + da * color + db * (1 - color)) % RING
        return px, py

    def column_block(da, db, color):
        px, py = place(da, db, color)
        return (px * RING + py) * 2 + color

    def peer(da, db):
        px, py = place(da % RING, db % RING, c)
        return (px, py, c, z)

    ways = {"a+": (1, 0), "a-": (-1, 0), "b+": (0, 1), "b-": (0, -1)}
    sibling = (x, y, other, z)
    up, down = (x, y, c, (z + 1) % DEPTH), (x, y, c, (z + DEPTH - 1) % DEPTH)
    neighbours = [peer(*step) for step in ways.values()] + [sibling, up, down]

    barrier = pltpu.get_barrier_semaphore()
    for neighbour in neighbours:
        pl.semaphore_signal(barrier, inc=1, device_id=neighbour, device_id_type=MESH)
    pl.semaphore_wait(barrier, len(neighbours))

    pending = []

    def remote(src, dst, send_sem, recv_sem, target):
        return pltpu.make_async_remote_copy(
            src_ref=src, dst_ref=dst, send_sem=send_sem, recv_sem=recv_sem,
            device_id=target, device_id_type=MESH,
        )

    def go(copy):
        copy.start()
        pending.append(copy)

    def part(index, h):
        return w.at[index, pl.ds(h * half, half), :]

    order = {name: place_at for place_at, name in enumerate(ways)}

    def push(da, db, h, way):
        step = ways[way]
        there = slot(da - step[0], db - step[1])
        here = slot(da, db)
        source = w_hbm.at[pl.ds(h * half, half), :] if here == 0 else part(here, h)
        go(remote(source, part(there, h), send.at[order[way] * 32 + here * 2 + h],
                  recv.at[there * 2 + h], peer(*step)))

    def across(da, db, h):
        here = slot(da, db)
        source = w_hbm.at[pl.ds(h * half, half), :] if here == 0 else part(here, h)
        go(remote(source, part(16 + here, h), sib_send.at[here * 2 + h],
                  sib_recv.at[here * 2 + h], sibling))

    def arrive(da, db, h, *onward):
        here = slot(da, db)
        ref = part(here, h)
        remote(ref, ref, send.at[0], recv.at[here * 2 + h], sibling).wait_recv()
        for way in onward:
            push(da, db, h, way)
        across(da, db, h)

    def sib_arrive(da, db):
        here = slot(da, db)
        for h in range(2):
            ref = part(16 + here, h)
            remote(ref, ref, send.at[0], sib_recv.at[here * 2 + h], sibling).wait_recv()

    def small_push(source, target_ref, k, way):
        go(remote(source, target_ref, s_send.at[k], s_recv.at[k], peer(*ways[way])))

    def small_arrive(ref, k):
        remote(ref, ref, s_send.at[0], s_recv.at[k], sibling).wait_recv()

    small_push(small_hbm, small.at[0, 0, 3], 0, "a+")
    small_push(small_hbm, small.at[0, 0, 1], 1, "a-")
    for h, one, two in ((0, "a+", "b+"), (1, "a-", "b-")):
        push(0, 0, h, one)
        push(0, 0, h, two)

    own_w = [pltpu.make_async_copy(w_hbm, w.at[0], local.at[0])]
    own_w[0].start()
    across(0, 0, 0)
    across(0, 0, 1)

    def z_block(ref, first, count):
        return ref.at[pl.ds(first, count)]

    z_own = z_block(bi, z * 4, 4)
    go(remote(bi_hbm, z_own, z_send.at[0], z_recv.at[0], up))
    go(remote(bi_hbm, z_own, z_send.at[1], z_recv.at[4], down))
    own_bi = pltpu.make_async_copy(bi_hbm, z_own, local.at[1])
    own_bi.start()
    own_small = pltpu.make_async_copy(small_hbm, small.at[0, 0, 0], local.at[2])
    own_small.start()
    own_bo = pltpu.make_async_copy(bo_hbm, bo, local.at[3])
    own_bo.start()
    own_seeds = pltpu.make_async_copy(seeds_hbm, seeds, local.at[4])
    own_seeds.start()

    loads = {}
    for color, at in ((c, 0), (other, 16)):
        for da in range(RING):
            for db in range(RING):
                start = pl.multiple_of(column_block(da, db, color) * 128, 128)
                index = at + slot(da, db)
                loads[index] = pltpu.make_async_copy(
                    tok_hbm.at[:, pl.ds(start, 128)], tok.at[index], tok_sem.at[index]
                )
    sequence = [(0, 0), (-1, 0), (1, 0), (0, -1), (0, 1), (2, 0), (-1, -1), (-1, 1), (1, -1),
                (1, 1), (0, 2), (2, -1), (2, 1), (-1, 2), (1, 2), (2, 2)]
    for place_at in sequence:
        for at in (0, 16):
            loads[at + slot(*place_at)].start()

    def blocks_of(places):
        return [at + slot(*place_at) for place_at in places for at in (0, 16)]

    def multiply(places, mode):
        blocks = blocks_of(places)
        for place_at in places:
            sib_arrive(*place_at)
        for block in blocks:
            loads[block].wait()
        lhs = [tok[block] for block in blocks]
        extra = mode == "term"
        if extra:
            lhs += [zz[0], zz[1]]
        lhs = jnp.concatenate(lhs, axis=1)

        @pl.loop(0, 2)
        def _(h):
            span = pl.ds(pl.multiple_of(h * half, half), half)
            rhs = [w[block, span, :] for block in blocks]
            if extra:
                rhs += [bo[span, :], bo[span, :]]
            product = nt(lhs, jnp.concatenate(rhs, axis=1))
            if mode == "first":
                acc[h] = product
            elif mode == "last":
                out[h] = (acc[h] + product).astype(BF16)
                start = pl.multiple_of(h * half, half)
                pltpu.make_async_copy(
                    out.at[h], hidden_hbm.at[:, pl.ds(start, half)], done.at[h]
                ).start()
            else:
                acc[h] += product

    def z_arrive(k, behind, first, count):
        block = (z + DEPTH - behind) % DEPTH * 4 + first
        ref = z_block(bi, block, count)
        remote(ref, ref, z_send.at[0], z_recv.at[k], sibling).wait_recv()

    def z_relay(k, behind, first, count, target):
        block = (z + DEPTH - behind) % DEPTH * 4 + first
        ref = z_block(bi, block, count)
        go(remote(ref, ref, z_send.at[k], z_recv.at[k], target))

    small_arrive(small.at[0, 0, 3], 0)
    small_push(small.at[0, 0, 3], small.at[0, 0, 2], 2, "a+")
    small_arrive(small.at[0, 0, 1], 1)
    for h, one, two in ((1, "a+", "b+"), (0, "a-", "b-")):
        push(0, 0, h, one)
        push(0, 0, h, two)
    own_w[0].wait()
    own_small.wait()
    own_bi.wait()
    own_bo.wait()
    own_seeds.wait()

    z_arrive(0, 1, 0, 4)
    z_relay(2, 1, 0, 4, up)
    z_arrive(4, 7, 0, 4)
    z_relay(5, 7, 0, 4, down)

    arrive(-1, 0, 0, "a+", "b+", "b-")
    arrive(1, 0, 1, "a-", "b+", "b-")
    small_arrive(small.at[0, 0, 2], 2)
    small_push(small.at[0, 0], small.at[0, 3], 3, "b+")
    small_push(small.at[0, 0], small.at[0, 1], 4, "b-")
    arrive(0, -1, 0, "b+")
    arrive(0, 1, 1, "b-")

    z_arrive(2, 2, 0, 4)
    z_relay(3, 2, 0, 4, up)
    z_arrive(5, 6, 0, 4)
    z_relay(6, 6, 0, 4, down)

    arrive(-1, 0, 1, "b+", "b-")
    arrive(1, 0, 0, "b+", "b-")
    arrive(0, -1, 1)
    arrive(0, 1, 0)
    small_arrive(small.at[0, 3], 3)
    small_push(small.at[0, 3], small.at[0, 2], 5, "b+")
    small_arrive(small.at[0, 1], 4)
    multiply([(0, 0), (-1, 0)], "first")
    arrive(2, 0, 0, "b+", "b-")
    arrive(2, 0, 1, "b+", "b-")
    z_arrive(3, 3, 0, 4)
    z_half_up = z_block(bi, (z + DEPTH - 3) % DEPTH * 4, 2)
    go(remote(z_half_up, z_half_up, z_send.at[4], z_recv.at[1], up))
    z_arrive(6, 5, 0, 4)
    z_half_down = z_block(bi, (z + DEPTH - 5) % DEPTH * 4 + 2, 2)
    go(remote(z_half_down, z_half_down, z_send.at[7], z_recv.at[7], down))
    multiply([(1, 0), (0, -1)], "add")
    arrive(-1, -1, 0, "b+")
    arrive(-1, 1, 0)
    arrive(1, -1, 1)
    arrive(1, 1, 1, "b-")
    small_arrive(small.at[0, 2], 5)
    go(remote(small.at[0], small.at[1], s_send.at[6], s_recv.at[6], sibling))
    arrive(0, 2, 0)
    arrive(0, 2, 1)
    multiply([(0, 1), (2, 0)], "add")
    z_arrive(1, 4, 0, 2)
    z_arrive(7, 4, 2, 2)
    small_arrive(small.at[1], 6)

    lanes = lax.broadcasted_iota(jnp.int32, (16, 128), 1)
    fit = [small[color, :, :, 8, :].reshape(16, 128).astype(F32) for color in range(2)]
    packed = jnp.where(lanes < 64, fit[0], fit[1])
    columns = jnp.concatenate([packed, jnp.zeros((112, 128), F32)], axis=0).T
    sums = [jnp.zeros((8, 128), F32) for _ in range(16)]
    for j in range(16):
        column = jnp.broadcast_to(columns[:, j : j + 1], (128, 128))
        for m in range(16):
            sign = jnp.clip(packed[m : m + 1, :] - column, -1.0, 1.0)
            sums[m] += jnp.sum(sign.reshape(16, 8, 128), axis=0)
    ranks = jnp.concatenate([jnp.sum(s, axis=0, keepdims=True) for s in sums], axis=0) + 512.0
    turned = pltpu.roll(ranks, 64, 1)
    for color in range(2):
        low, high = (ranks, turned) if color == 0 else (turned, ranks)
        both = jnp.where(lanes < 64, low, high)
        coarse = jnp.floor(both * (1.0 / 16.0)) * 16.0
        weights[color, 0] = coarse
        weights[color, 1] = both - coarse

    arrive(-1, -1, 1)
    arrive(-1, 1, 1, "b-")
    arrive(1, -1, 0, "b+")
    arrive(1, 1, 0)

    levels = lax.broadcasted_iota(jnp.int32, (128, 128), 0)
    coup[...] = jnp.zeros_like(coup)

    def couple(color):
        @pl.loop(0, 16)
        def _(r):
            block = small[color, r // RING, r % RING]
            coarse = weights[color, 0, pl.ds(r, 1), :]
            fine = weights[color, 1, pl.ds(r, 1), :]
            hits, tops, rests = [], [], []
            for j in range(4):
                hits.append(one_hot_row(levels, block[j : j + 1]).astype(F32).astype(BF16))
                hit = one_hot_row(levels, block[4 + j : 5 + j])
                tops.append(jnp.where(hit, coarse, 0.0).astype(BF16))
                rests.append(jnp.where(hit, fine, 0.0).astype(BF16))
            rhs = jnp.concatenate(
                [jnp.concatenate(tops, axis=1), jnp.concatenate(rests, axis=1)], axis=0
            )
            coup[...] += nt(jnp.concatenate(hits, axis=1), rhs)

    couple(0)
    arrive(2, -1, 0, "b+")
    arrive(2, 1, 0)
    couple(1)
    arrive(2, -1, 1)
    arrive(2, 1, 1, "b-")
    multiply([(-1, -1), (-1, 1)], "add")

    coupling = (coup[:, :128] + coup[:, 128:]) * (STEP_SCALE / (2.0 * (16 * 96 - 1)))
    c_high, c_low = halves(coupling)
    own_in = bi[column_block(0, 0, c)]
    m_high, m_low = halves(nt(c_high, own_in) + nt(c_low, own_in))
    update = nn(jnp.concatenate([bo[...], bo[...]], axis=1), jnp.concatenate([m_high, m_low], axis=0))
    nw[...] = (w[0].astype(F32) + update).astype(BF16)
    nw_copy = pltpu.make_async_copy(nw, nw_hbm, done.at[2])
    nw_copy.start()
    multiply([(1, -1), (1, 1)], "add")
    arrive(-1, 2, 0)
    arrive(-1, 2, 1)

    def project(g, total):
        lhs, rhs = [], []
        for db in range(RING):
            color = (c + g // RING) % 2
            lhs.append(tok[g * RING + db])
            rhs.append(bi[column_block(g % RING, db, color)])
        return total + nn(jnp.concatenate(lhs, axis=1), jnp.concatenate(rhs, axis=0))

    for place_at in [(0, 2), (2, -1), (2, 1), (-1, 2), (1, 2), (2, 2)]:
        for at in (0, 16):
            loads[at + slot(*place_at)].wait()
            loads[at + slot(*place_at)] = None
    tokens = tok.shape[1]
    projected = lax.fori_loop(0, 2 * RING, project, jnp.zeros((tokens, 128), F32))
    p_high, p_low = halves(projected)
    outs, ins = [], []
    for j in range(4):
        outs.append(one_hot_row(levels, seeds[j : j + 1]).astype(F32).astype(BF16))
        ins.append(one_hot_row(levels, seeds[4 + j : 5 + j]).astype(F32).astype(BF16))
    ins = jnp.concatenate(ins, axis=1)
    picked = nn(jnp.concatenate([p_high, p_low], axis=1), jnp.concatenate([ins, ins], axis=0))
    member = lax.shift_right_logical(lax.broadcasted_iota(jnp.int32, picked.shape, 0), 4)
    lane = lax.broadcasted_iota(jnp.int32, picked.shape, 1) & 63
    g_high, g_low = halves(jnp.where(member == lane, picked * NOISE_SCALE, 0.0))
    term = nt(
        jnp.concatenate([p_high, p_low, p_high, g_high, g_low], axis=1),
        jnp.concatenate([c_high, c_high, c_low, *outs, *outs], axis=1),
    )
    z_high, z_low = halves(term)
    zz[0] = z_high
    zz[1] = z_low

    arrive(1, 2, 0)
    arrive(1, 2, 1)

    class Ready:
        def wait(self):
            pass

    for key in loads:
        loads[key] = loads[key] or Ready()
    multiply([(0, 2), (2, -1)], "term")
    arrive(2, 2, 0)
    arrive(2, 2, 1)
    multiply([(2, 1), (-1, 2)], "add")
    multiply([(1, 2), (2, 2)], "last")

    for copy in pending:
        copy.wait_send()
    nw_copy.wait()
    for h in range(2):
        pltpu.make_async_copy(out.at[h], hidden_hbm.at[:, pl.ds(h * half, half)], done.at[h]).wait()


def lane_packed(seeds):
    pairs = seeds.transpose(1, 2, 0).reshape(2, 4, 2, seeds.shape[0])
    pairs = jnp.pad(pairs, ((0, 0), (0, 0), (0, 0), (0, 64 - seeds.shape[0])), constant_values=-1)
    return pairs.reshape(8, 128)


def shards(tokens, weight, bank_in, bank_out, fitness, past_seeds, new_seeds):
    members, each, features = tokens.shape
    rows, wide = weight.shape
    flat = members * each
    levels = jnp.pad(
        jnp.broadcast_to(fitness, (2, members)), ((0, 0), (0, 64 - members)), constant_values=FAR
    ).reshape(1, 128)
    small = jnp.concatenate(
        [lane_packed(past_seeds), jnp.broadcast_to(levels, (8, 128))], axis=0
    )
    dma = pltpu.SemaphoreType.DMA
    hidden, new_weight = pl.pallas_call(
        kernel,
        out_shape=(
            jax.ShapeDtypeStruct((flat, rows), BF16),
            jax.ShapeDtypeStruct((rows, wide), BF16),
        ),
        in_specs=[pl.BlockSpec(memory_space=pl.ANY)] * 6,
        out_specs=[pl.BlockSpec(memory_space=pl.ANY)] * 2,
        scratch_shapes=[
            pltpu.VMEM((32, flat, 128), BF16),
            pltpu.VMEM((32, rows, 128), BF16),
            pltpu.VMEM((32, 128, 128), BF16),
            pltpu.VMEM((rows, 128), BF16),
            pltpu.VMEM((2, RING, RING, 16, 128), jnp.int32),
            pltpu.VMEM((8, 128), jnp.int32),
            pltpu.VMEM((2, flat, rows // 2), F32),
            pltpu.VMEM((2, flat, rows // 2), BF16),
            pltpu.VMEM((rows, 128), BF16),
            pltpu.VMEM((2, 2, 16, 128), F32),
            pltpu.VMEM((128, 256), F32),
            pltpu.VMEM((2, flat, 128), BF16),
            dma((128,)), dma((32,)), dma((32,)), dma((32,)), dma((8,)), dma((8,)),
            dma((7,)), dma((7,)), dma((32,)), dma((5,)), dma((3,)),
        ],
        compiler_params=pltpu.CompilerParams(
            collective_id=0, has_side_effects=True, vmem_limit_bytes=60 * 1024 * 1024
        ),
    )(
        tokens.reshape(flat, features), weight, bank_in.reshape(4, 128, 128), bank_out,
        small, lane_packed(new_seeds),
    )
    return hidden.reshape(members, each, rows), new_weight


def solution(mesh):
    torus = Mesh(
        mesh.devices.reshape(4, 4, 2, mesh.shape["row"]), ("pop_0", "pop_1", "pop_2", "row")
    )
    return jax.shard_map(
        shards,
        mesh=torus,
        in_specs=(
            P(POP, None, None),
            P("row", POP),
            P("row", None),
            P("row", None),
            P(POP),
            P(POP, None, None),
            P(POP, None, None),
        ),
        out_specs=(P(POP, None, "row"), P("row", POP)),
        check_vma=False,
    )
```

time: 147 us -> 76.4 us (0.52)
  Pallas kernels: 0 us -> 67.7 us
  matrix products: 37.5 us -> 0 us
  blocking collectives: 34.4 us -> 0 us
  waiting for transfers between devices: 30.1 us -> 0 us
  starting transfers between devices: 16.8 us -> 0 us
  between operations: 16.2 us -> 0.65 us
  local copies, waits for them, and re-layouts: 9.53 us -> 7.23 us
    pallas_call x0 -> x1, Pallas kernels: none -> 67.7 us  [shards(): pl.pallas_call(kernel, out_shape=(jax.ShapeDtypeStruct((flat, rows), BF16...]
    dot_general x6 -> x0, matrix products: 37.5 us -> none  [the longest x1 23.6 us: shards(): lax.dot_general(columns, refresh(lax.all_gather(weight, POP, axis=1, tile...]
    all_gather x3 -> x0, blocking collectives: 20.7 us -> none  [all_blocks(): blocks = lax.all_gather(blocks, axes[k], axis=0, tiled=True)]
    all_to_all x2 -> x0, starting transfers between devices: 16.8 us -> none  [sent_to_all(): lax.all_to_all(jnp.broadcast_to(array[None], (count, *array.shape)), axis...]
    all_gather x1 -> x0, waiting for transfers between devices: 15.8 us -> none  [shards(): lax.all_gather(weight, POP, axis=1, tiled=True)]
    unnamed x2 -> x0, blocking collectives: 13.8 us -> none
    reduce_scatter x1 -> x0, waiting for transfers between devices: 7.64 us -> none  [own_block(): blocks = lax.psum_scatter(blocks, axes[k], scatter_dimension=0, tiled=True)]
    all_to_all x2 -> x0, waiting for transfers between devices: 6.14 us -> none  [sent_to_all(): lax.all_to_all(jnp.broadcast_to(array[None], (count, *array.shape)), axis...]
  transfers between devices with their start and end apart: 4 -> 0, of which waited for: 3 -> 0; matrix products, arithmetic and copies ran while one was open for 11% -> 0% of each run, Pallas kernels for 0% -> 0%
where the time goes in v1:
time: 76.4 us; the launch traced here: 76.2 us
  Pallas kernels  67.7 us (89%)
  local copies, waits for them, and re-layouts  7.23 us (9%)
    pallas_call x1, Pallas kernels, shards(): pl.pallas_call(kernel, out_shape=(jax.ShapeDtypeStruct((flat, rows), BF16...  67.7 us
    unnamed x4, local copies, waits for them, and re-layouts  4.31 us

profile of v1, /device:TPU:1, one launch (start us, length us, event | category | flops | bytes accessed | tf_op | source)
XLA Modules:
  0.0 76.2 jit_solution(9102501495555517926)
XLA Ops:
  0.6 0.7 pad.14
  1.3 0.1 broadcast_in_dim.8
  1.4 0.7 pad.13
  2.1 0.1 reshape.30
  2.2 0.6 pad_add_fusion.small_hbm
  2.8 0.7 pad.16
  3.5 0.7 reshape.32.seeds_hbm
  4.1 67.7 %shard_map.86 = (bf16[768,1792]{1,0:T(8,128)(2,1)}, bf16[1792,128]{1,0:T(8,128)(2,1)}) custom-call(bf16[768,4096]{1,0:T(8,128)(2,1)} %bitcast.9, bf16[1792,128]{1,0:T(8,128)(2,1)} %w_hbm.1, bf16[4,128,128]{2,1,0:T(8,128)(2,1)} %bitcast.11, bf16[1792,128]{1,0:T(8,128)(2,1)} %bo_hbm.1, s32[16,128]{1,0:T(8,128)} %pad_add_fusion.small_hbm, ...), custom_call_target="tpu_custom_call" | custom-call | tf_op jit(solution)/shard_map/pallas_call | solution.py:409
  71.8 0.0 copy-start
  71.9 3.5 %copy.11 = bf16[48,16,1792]{2,1,0:T(8,128)(2,1)} copy(bf16[48,16,1792]{2,1,0:T(8,128)(2,1)} %bitcast.10) | data formatting | bytes 5505024
  75.4 0.0 copy-done
  75.4 0.8 %copy.12 = bf16[1792,128]{1,0:T(8,128)(2,1)} copy(bf16[1792,128]{1,0:T(8,128)(2,1)S(1)} %copy-done) | data formatting | bytes 917504
  (2 shorter events, 0.0 us)
Async XLA Ops:
  71.8 3.6 %copy-start = (bf16[1792,128]{1,0:T(8,128)(2,1)S(1)}, bf16[1792,128]{1,0:T(8,128)(2,1)}, u32[]{:S(2)}) copy-start(bf16[1792,128]{1,0:T(8,128)(2,1)} %get-tuple-element.9) | copy-start | bytes 1376260

commit v2 on v1

v2 whole, which is shorter than its diff:
```python
import functools

import jax
import jax.numpy as jnp
from jax import lax
from jax.experimental import pallas as pl
from jax.experimental.pallas import tpu as pltpu
from jax.sharding import Mesh
from jax.sharding import PartitionSpec as P

POP = ("pop_0", "pop_1", "pop_2")
MESH = pl.DeviceIdType.MESH

NOISE_SCALE = 0.1
STEP_SCALE = 0.03

RING = 4
DEPTH = 8
FAR = 1 << 20
F32 = jnp.float32
BF16 = jnp.bfloat16


def nt(a, b):
    return lax.dot_general(a, b, (((1,), (1,)), ((), ())), preferred_element_type=F32)


def nn(a, b):
    return jnp.dot(a, b, preferred_element_type=F32)


def halves(a):
    high = a.astype(BF16)
    return high, (a - high.astype(F32)).astype(BF16)


def slot(da, db):
    return (da % RING) * RING + db % RING


def one_hot_row(levels, row):
    return levels == jnp.broadcast_to(row, levels.shape)


def kernel(
    tok_hbm, w_hbm, bi_hbm, bo_hbm, fit_hbm, past_hbm, seeds_hbm, out, nw,
    tok, w, bi, bo, past, fit, seeds, acc, weights, coup, shares, zz,
    send, recv, sib_send, sib_recv, z_send, z_recv, s_send, s_recv, tok_sem, local,
):
    x, y, c, z = (lax.axis_index(name) for name in (*POP, "row"))
    rows = w_hbm.shape[0]
    half = rows // 2
    other = 1 - c

    def place(da, db, color):
        px = (x + da * (1 - color) + db * color) % RING
        py = (y + da * color + db * (1 - color)) % RING
        return px, py

    def column_block(da, db, color):
        px, py = place(da, db, color)
        return (px * RING + py) * 2 + color

    def peer(da, db):
        px, py = place(da % RING, db % RING, c)
        return (px, py, c, z)

    ways = {"a+": (1, 0), "a-": (-1, 0), "b+": (0, 1), "b-": (0, -1)}
    sibling = (x, y, other, z)
    up, down = (x, y, c, (z + 1) % DEPTH), (x, y, c, (z + DEPTH - 1) % DEPTH)
    neighbours = [peer(*step) for step in ways.values()] + [sibling, up, down]

    barrier = pltpu.get_barrier_semaphore()
    for neighbour in neighbours:
        pl.semaphore_signal(barrier, inc=1, device_id=neighbour, device_id_type=MESH)
    pl.semaphore_wait(barrier, len(neighbours))

    pending = []

    def remote(src, dst, send_sem, recv_sem, target):
        return pltpu.make_async_remote_copy(
            src_ref=src, dst_ref=dst, send_sem=send_sem, recv_sem=recv_sem,
            device_id=target, device_id_type=MESH,
        )

    def go(copy):
        copy.start()
        pending.append(copy)

    def part(index, h):
        return w.at[index, pl.ds(h * half, half), :]

    order = {name: place_at for place_at, name in enumerate(ways)}

    def push(da, db, h, way):
        step = ways[way]
        there = slot(da - step[0], db - step[1])
        here = slot(da, db)
        source = w_hbm.at[pl.ds(h * half, half), :] if here == 0 else part(here, h)
        go(remote(source, part(there, h), send.at[order[way] * 32 + here * 2 + h],
                  recv.at[there * 2 + h], peer(*step)))

    def across(da, db, h):
        here = slot(da, db)
        source = w_hbm.at[pl.ds(h * half, half), :] if here == 0 else part(here, h)
        go(remote(source, part(16 + here, h), sib_send.at[here * 2 + h],
                  sib_recv.at[here * 2 + h], sibling))

    def arrive(da, db, h, *onward):
        here = slot(da, db)
        ref = part(here, h)
        remote(ref, ref, send.at[0], recv.at[here * 2 + h], sibling).wait_recv()
        for way in onward:
            push(da, db, h, way)
        across(da, db, h)

    def sib_arrive(da, db):
        here = slot(da, db)
        for h in range(2):
            ref = part(16 + here, h)
            remote(ref, ref, send.at[0], sib_recv.at[here * 2 + h], sibling).wait_recv()

    def small_push(k, way, first, there, count):
        for j, (ref, own) in enumerate(((past, past_hbm), (fit, fit_hbm))):
            if count == 1:
                source = own if first == 0 else ref.at[0, first]
                target = ref.at[0, there]
            else:
                source = ref.at[0, pl.ds(first, count)]
                target = ref.at[0, pl.ds(there, count)]
            go(remote(source, target, s_send.at[2 * k + j], s_recv.at[2 * k + j],
                      peer(*ways[way])))

    def small_arrive(k, there, count):
        for j, ref in enumerate((past, fit)):
            ref = ref.at[0, there] if count == 1 else ref.at[0, pl.ds(there, count)]
            remote(ref, ref, s_send.at[0], s_recv.at[2 * k + j], sibling).wait_recv()

    small_push(0, "a+", 0, 3, 1)
    small_push(1, "a-", 0, 1, 1)
    for h, one, two in ((0, "a+", "b+"), (1, "a-", "b-")):
        push(0, 0, h, one)
        push(0, 0, h, two)

    own_w = [pltpu.make_async_copy(w_hbm, w.at[0], local.at[0])]
    own_w[0].start()
    across(0, 0, 0)
    across(0, 0, 1)

    def z_block(ref, first, count):
        return ref.at[pl.ds(first, count)]

    z_own = z_block(bi, z * 4, 4)
    go(remote(bi_hbm, z_own, z_send.at[0], z_recv.at[0], up))
    go(remote(bi_hbm, z_own, z_send.at[1], z_recv.at[4], down))
    own_bi = pltpu.make_async_copy(bi_hbm, z_own, local.at[1])
    own_bi.start()
    own_past = pltpu.make_async_copy(past_hbm, past.at[0, 0], local.at[2])
    own_past.start()
    own_fit = pltpu.make_async_copy(fit_hbm, fit.at[0, 0], local.at[5])
    own_fit.start()
    own_bo = pltpu.make_async_copy(bo_hbm, bo, local.at[3])
    own_bo.start()
    own_seeds = pltpu.make_async_copy(seeds_hbm, seeds, local.at[4])
    own_seeds.start()

    loads = {}
    for color, at in ((c, 0), (other, 16)):
        for da in range(RING):
            for db in range(RING):
                start = pl.multiple_of(column_block(da, db, color) * 128, 128)
                index = at + slot(da, db)
                loads[index] = pltpu.make_async_copy(
                    tok_hbm.at[:, pl.ds(start, 128)], tok.at[index], tok_sem.at[index]
                )
    sequence = [(0, 0), (-1, 0), (1, 0), (0, -1), (0, 1), (2, 0), (0, 2), (-1, -1), (-1, 1),
                (1, -1), (1, 1), (2, -1), (2, 1), (-1, 2), (1, 2), (2, 2)]
    for place_at in sequence:
        for at in (0, 16):
            loads[at + slot(*place_at)].start()

    def blocks_of(places):
        return [at + slot(*place_at) for place_at in places for at in (0, 16)]

    def multiply(places, mode):
        blocks = blocks_of(places)
        for place_at in places:
            sib_arrive(*place_at)
        for block in blocks:
            if block in loads:
                loads.pop(block).wait()
        lhs = [tok[block] for block in blocks]
        extra = mode == "term"
        if extra:
            lhs += [zz[0], zz[1]]
        lhs = jnp.concatenate(lhs, axis=1)

        @pl.loop(0, 2)
        def _(h):
            span = pl.ds(pl.multiple_of(h * half, half), half)
            rhs = [w[block, span, :] for block in blocks]
            if extra:
                rhs += [bo[span, :], bo[span, :]]
            product = nt(lhs, jnp.concatenate(rhs, axis=1))
            if mode == "first":
                acc[h] = product
            elif mode == "last":
                out[:, span] = (acc[h] + product).astype(BF16)
            else:
                acc[h] += product

    def z_arrive(k, behind, first, count):
        block = (z + DEPTH - behind) % DEPTH * 4 + first
        ref = z_block(bi, block, count)
        remote(ref, ref, z_send.at[0], z_recv.at[k], sibling).wait_recv()

    def z_relay(k, behind, first, count, target):
        block = (z + DEPTH - behind) % DEPTH * 4 + first
        ref = z_block(bi, block, count)
        go(remote(ref, ref, z_send.at[k], z_recv.at[k], target))

    lanes = lax.broadcasted_iota(jnp.int32, (8, 128), 1)

    def padded(rows, filler):
        return jnp.concatenate(
            [rows, jnp.full((rows.shape[0], 128 - rows.shape[1]), filler, rows.dtype)], axis=1
        )

    def paired(rows):
        rows = padded(rows, -1)
        return jnp.where(lanes < 64, rows, pltpu.roll(pltpu.roll(rows, 4, 0), 64, 1))

    small_arrive(0, 3, 1)
    small_push(2, "a+", 3, 2, 1)
    small_arrive(1, 1, 1)
    for h, one, two in ((1, "a+", "b+"), (0, "a-", "b-")):
        push(0, 0, h, one)
        push(0, 0, h, two)
    own_w[0].wait()
    own_past.wait()
    own_fit.wait()
    own_bi.wait()
    own_bo.wait()
    own_seeds.wait()
    multiply([(0, 0)], "first")

    small_arrive(2, 2, 1)
    small_push(3, "b+", 0, 12, 4)
    small_push(4, "b-", 0, 4, 4)
    z_arrive(0, 1, 0, 4)
    z_relay(2, 1, 0, 4, up)
    z_arrive(4, 7, 0, 4)
    z_relay(5, 7, 0, 4, down)

    arrive(-1, 0, 0, "a+", "b+", "b-")
    arrive(1, 0, 1, "a-", "b+", "b-")
    arrive(0, -1, 0, "b+")
    arrive(0, 1, 1, "b-")

    z_arrive(2, 2, 0, 4)
    z_relay(3, 2, 0, 4, up)
    z_arrive(5, 6, 0, 4)
    z_relay(6, 6, 0, 4, down)
    small_arrive(3, 12, 4)
    small_push(5, "b+", 12, 8, 4)
    small_arrive(4, 4, 4)

    arrive(-1, 0, 1, "b+", "b-")
    arrive(1, 0, 0, "b+", "b-")
    arrive(0, -1, 1)
    arrive(0, 1, 0)
    z_arrive(3, 3, 0, 4)
    z_half_up = z_block(bi, (z + DEPTH - 3) % DEPTH * 4, 2)
    go(remote(z_half_up, z_half_up, z_send.at[4], z_recv.at[1], up))
    z_arrive(6, 5, 0, 4)
    z_half_down = z_block(bi, (z + DEPTH - 5) % DEPTH * 4 + 2, 2)
    go(remote(z_half_down, z_half_down, z_send.at[7], z_recv.at[7], down))
    multiply([(-1, 0), (1, 0)], "add")
    small_arrive(5, 8, 4)
    go(remote(fit.at[0], fit.at[1], s_send.at[12], s_recv.at[12], sibling))
    multiply([(0, -1), (0, 1)], "add")
    arrive(2, 0, 0, "b+", "b-")
    arrive(2, 0, 1, "b+", "b-")
    arrive(-1, -1, 0, "b+")
    arrive(-1, 1, 0)

    remote(fit.at[0], fit.at[1], s_send.at[12], s_recv.at[12], sibling).wait_recv()
    wide = lax.broadcasted_iota(jnp.int32, (16, 128), 1)
    mine, theirs = (
        padded(jnp.concatenate([fit[k, r] for r in range(16)], axis=0), FAR).astype(F32)
        for k in range(2)
    )
    everyone = jnp.where(wide < 64, mine, pltpu.roll(theirs, 64, 1))
    columns = jnp.concatenate([everyone, jnp.zeros((112, 128), F32)], axis=0).T
    packed = jnp.where(lanes < 64, mine[:8], pltpu.roll(mine[8:], 64, 1))
    sums = [jnp.zeros((8, 128), F32) for _ in range(8)]
    for j in range(16):
        column = jnp.broadcast_to(columns[:, j : j + 1], (128, 128))
        for m in range(8):
            sign = jnp.clip(packed[m : m + 1, :] - column, -1.0, 1.0)
            sums[m] += jnp.sum(sign.reshape(16, 8, 128), axis=0)
    ranks = jnp.concatenate([jnp.sum(s, axis=0, keepdims=True) for s in sums], axis=0) + 512.0
    turned = pltpu.roll(ranks, 64, 1)
    for first, low, high in ((0, ranks, turned), (8, turned, ranks)):
        both = jnp.where(lanes < 64, low, high)
        coarse = jnp.floor(both * (1.0 / 16.0)) * 16.0
        weights[0, first : first + 8] = coarse
        weights[1, first : first + 8] = both - coarse

    arrive(1, -1, 1)
    arrive(1, 1, 1, "b-")

    levels = lax.broadcasted_iota(jnp.int32, (128, 128), 0)

    def hot(rows):
        return [one_hot_row(levels, rows[j : j + 1]).astype(F32).astype(BF16) for j in range(4)]

    coup[...] = jnp.zeros_like(coup)

    def couple(first, last):
        @pl.loop(first, last)
        def _(r):
            coarse = weights[0, pl.ds(r, 1), :]
            fine = weights[1, pl.ds(r, 1), :]
            features = paired(past[0, r, 1])
            tops, rests = [], []
            for j in range(4):
                hit = one_hot_row(levels, features[j : j + 1])
                tops.append(jnp.where(hit, coarse, 0.0).astype(BF16))
                rests.append(jnp.where(hit, fine, 0.0).astype(BF16))
            lhs = jnp.concatenate(
                [jnp.concatenate(tops, axis=1), jnp.concatenate(rests, axis=1)], axis=0
            )
            coup[...] += nt(lhs, jnp.concatenate(hot(paired(past[0, r, 0])), axis=1))

    couple(0, 8)
    arrive(0, 2, 0)
    arrive(0, 2, 1)
    couple(8, 16)
    shares[0] = coup[:128, :] + coup[128:, :]
    arrive(-1, -1, 1)
    arrive(-1, 1, 1, "b-")
    multiply([(2, 0), (0, 2)], "add")
    go(remote(shares.at[0], shares.at[1], s_send.at[13], s_recv.at[13], sibling))
    arrive(1, -1, 0, "b+")
    arrive(1, 1, 0)
    multiply([(-1, -1), (-1, 1)], "add")
    z_arrive(1, 4, 0, 2)
    z_arrive(7, 4, 2, 2)

    for block in sorted(loads):
        loads.pop(block).wait()
    def project(g, total):
        lhs, rhs = [], []
        for db in range(RING):
            color = (c + g // RING) % 2
            lhs.append(tok[g * RING + db])
            rhs.append(bi[column_block(g % RING, db, color)])
        return total + nn(jnp.concatenate(lhs, axis=1), jnp.concatenate(rhs, axis=0))

    tokens = tok.shape[1]
    projected = lax.fori_loop(0, 2 * RING, project, jnp.zeros((tokens, 128), F32))
    p_high, p_low = halves(projected)
    arrive(2, -1, 0, "b+")
    arrive(2, 1, 0)
    multiply([(1, -1), (1, 1)], "add")

    remote(shares.at[0], shares.at[1], s_send.at[13], s_recv.at[13], sibling).wait_recv()
    coupling = ((shares[0] + shares[1]) * (STEP_SCALE / (2.0 * (16 * 96 - 1)))).T
    c_high, c_low = halves(coupling)
    own_in = bi[column_block(0, 0, c)]
    m_high, m_low = halves(nt(c_high, own_in) + nt(c_low, own_in))
    update = nn(jnp.concatenate([bo[...], bo[...]], axis=1), jnp.concatenate([m_high, m_low], axis=0))
    nw[...] = (w[0].astype(F32) + update).astype(BF16)
    arrive(2, -1, 1)
    arrive(2, 1, 1, "b-")

    outs, ins = hot(paired(seeds[0])), jnp.concatenate(hot(paired(seeds[1])), axis=1)
    picked = nn(jnp.concatenate([p_high, p_low], axis=1), jnp.concatenate([ins, ins], axis=0))
    member = lax.shift_right_logical(lax.broadcasted_iota(jnp.int32, picked.shape, 0), 4)
    lane = lax.broadcasted_iota(jnp.int32, picked.shape, 1) & 63
    g_high, g_low = halves(jnp.where(member == lane, picked * NOISE_SCALE, 0.0))
    term = nt(
        jnp.concatenate([p_high, p_low, p_high, g_high, g_low], axis=1),
        jnp.concatenate([c_high, c_high, c_low, *outs, *outs], axis=1),
    )
    z_high, z_low = halves(term)
    zz[0] = z_high
    zz[1] = z_low
    multiply([(2, -1), (2, 1)], "term")
    arrive(-1, 2, 0)
    arrive(-1, 2, 1)
    arrive(1, 2, 0)
    arrive(1, 2, 1)
    multiply([(-1, 2), (1, 2)], "add")
    arrive(2, 2, 0)
    arrive(2, 2, 1)
    multiply([(2, 2)], "last")

    for copy in pending:
        copy.wait_send()


def shards(tokens, weight, bank_in, bank_out, fitness, past_seeds, new_seeds):
    members, each, features = tokens.shape
    rows, wide = weight.shape
    flat = members * each
    seeds = (*past_seeds.shape[1:], members)
    dma = pltpu.SemaphoreType.DMA
    hidden, new_weight = pl.pallas_call(
        kernel,
        out_shape=(
            pltpu.VMEM((flat, rows), BF16),
            pltpu.VMEM((rows, wide), BF16),
        ),
        in_specs=[pl.BlockSpec(memory_space=pl.ANY)] * 7,
        out_specs=[pl.BlockSpec(memory_space=pltpu.VMEM)] * 2,
        scratch_shapes=[
            pltpu.VMEM((32, flat, 128), BF16),
            pltpu.VMEM((32, rows, 128), BF16),
            pltpu.VMEM((32, 128, 128), BF16),
            pltpu.VMEM((rows, 128), BF16),
            pltpu.VMEM((2, 16, *seeds), jnp.int32),
            pltpu.VMEM((2, 16, 1, members), jnp.int32),
            pltpu.VMEM(seeds, jnp.int32),
            pltpu.VMEM((2, flat, rows // 2), F32),
            pltpu.VMEM((2, 16, 128), F32),
            pltpu.VMEM((256, 128), F32),
            pltpu.VMEM((2, 128, 128), F32),
            pltpu.VMEM((2, flat, 128), BF16),
            dma((128,)), dma((32,)), dma((32,)), dma((32,)), dma((8,)), dma((8,)),
            dma((14,)), dma((14,)), dma((32,)), dma((6,)),
        ],
        compiler_params=pltpu.CompilerParams(
            collective_id=0, has_side_effects=True, vmem_limit_bytes=56 * 1024 * 1024
        ),
    )(
        tokens.reshape(flat, features), weight, bank_in.reshape(4, 128, 128), bank_out,
        fitness.reshape(1, members), past_seeds.transpose(1, 2, 0), new_seeds.transpose(1, 2, 0),
    )
    return hidden.reshape(members, each, rows), new_weight


def solution(mesh):
    torus = Mesh(
        mesh.devices.reshape(4, 4, 2, mesh.shape["row"]), ("pop_0", "pop_1", "pop_2", "row")
    )
    return jax.shard_map(
        shards,
        mesh=torus,
        in_specs=(
            P(POP, None, None),
            P("row", POP),
            P("row", None),
            P("row", None),
            P(POP),
            P(POP, None, None),
            P(POP, None, None),
        ),
        out_specs=(P(POP, None, "row"), P("row", POP)),
        check_vma=False,
    )
```

time: 76.4 us -> 68 us (0.89)
  local copies, waits for them, and re-layouts: 7.23 us -> 2.3 us
  Pallas kernels: 67.7 us -> 65 us
    pallas_call x1, Pallas kernels: 67.7 us -> 65 us  [shards(): pl.pallas_call(kernel, out_shape=(pltpu.VMEM((flat, rows), BF16), pltpu.V...]
    pad x4 -> x0, local copies, waits for them, and re-layouts: 2.07 us -> none  [the longest x2 1.41 us: lane_packed(): jnp.pad(pairs, ((0, 0), (0, 0), (0, 0), (0, 64 - seeds.shape[0])), consta...]
    unnamed x4 -> x2, local copies, waits for them, and re-layouts: 4.31 us -> 2.3 us
where the time goes in v2:
time: 68 us; the launch traced here: 67.9 us
  Pallas kernels  65 us (96%)
  local copies, waits for them, and re-layouts  2.3 us (3%)
    pallas_call x1, Pallas kernels, shards(): pl.pallas_call(kernel, out_shape=(pltpu.VMEM((flat, rows), BF16), pltpu.V...  65 us
    unnamed x2, local copies, waits for them, and re-layouts  2.3 us

profile of v2, /device:TPU:1, one launch (start us, length us, event | category | flops | bytes accessed | tf_op | source)
XLA Modules:
  0.0 67.9 jit_solution(1803837490909737771)
XLA Ops:
  0.6 65.0 %shard_map.86 = (bf16[768,1792]{1,0:T(8,128)(2,1)S(1)}, bf16[1792,128]{1,0:T(8,128)(2,1)S(1)}) custom-call(bf16[768,4096]{1,0:T(8,128)(2,1)} %bitcast.7, bf16[1792,128]{1,0:T(8,128)(2,1)} %w_hbm.1, bf16[4,128,128]{2,1,0:T(8,128)(2,1)} %bitcast.8, bf16[1792,128]{1,0:T(8,128)(2,1)} %bo_hbm.1, s32[1,48]{1,0:T(1,128)} %bitcast.11, s32[2,8,48]{2,1,0:T(8,128)} %bitcast.9, ...), custom_call_target="tpu_custom_call" | custom-call | tf_op jit(solution)/shard_map/pallas_call | solution.py:410
  65.6 1.5 %copy.11 = bf16[48,16,1792]{2,1,0:T(8,128)(2,1)} copy(bf16[48,16,1792]{2,1,0:T(8,128)(2,1)S(1)} %bitcast.6) | data formatting | bytes 5505024
  67.1 0.8 %copy.12 = bf16[1792,128]{1,0:T(8,128)(2,1)} copy(bf16[1792,128]{1,0:T(8,128)(2,1)S(1)} %get-tuple-element.7) | data formatting | bytes 917504

commit v3 on v2

--- a/solution.py
+++ b/solution.py
@@ -138,9 +138,8 @@
 
     small_push(0, "a+", 0, 3, 1)
     small_push(1, "a-", 0, 1, 1)
-    for h, one, two in ((0, "a+", "b+"), (1, "a-", "b-")):
-        push(0, 0, h, one)
-        push(0, 0, h, two)
+    push(0, 0, 0, "a+")
+    push(0, 0, 1, "a-")
 
     own_w = [pltpu.make_async_copy(w_hbm, w.at[0], local.at[0])]
     own_w[0].start()
@@ -233,56 +232,47 @@
     small_arrive(0, 3, 1)
     small_push(2, "a+", 3, 2, 1)
     small_arrive(1, 1, 1)
-    for h, one, two in ((1, "a+", "b+"), (0, "a-", "b-")):
-        push(0, 0, h, one)
-        push(0, 0, h, two)
-    own_w[0].wait()
+    push(0, 0, 1, "a+")
+    push(0, 0, 0, "a-")
     own_past.wait()
     own_fit.wait()
+    small_arrive(2, 2, 1)
+    small_push(3, "b+", 0, 12, 4)
+    small_push(4, "b-", 0, 4, 4)
+    push(0, 0, 0, "b+")
+    push(0, 0, 1, "b-")
+    arrive(-1, 0, 0, "a+")
+    arrive(1, 0, 1, "a-")
+    own_w[0].wait()
     own_bi.wait()
     own_bo.wait()
     own_seeds.wait()
     multiply([(0, 0)], "first")
-
-    small_arrive(2, 2, 1)
-    small_push(3, "b+", 0, 12, 4)
-    small_push(4, "b-", 0, 4, 4)
+    small_arrive(3, 12, 4)
+    small_push(5, "b+", 12, 8, 4)
+    small_arrive(4, 4, 4)
+    push(0, 0, 1, "b+")
+    push(0, 0, 0, "b-")
+    for da, h in ((-1, 0), (1, 1)):
+        push(da, 0, h, "b+")
+        push(da, 0, h, "b-")
     z_arrive(0, 1, 0, 4)
     z_relay(2, 1, 0, 4, up)
     z_arrive(4, 7, 0, 4)
     z_relay(5, 7, 0, 4, down)
-
-    arrive(-1, 0, 0, "a+", "b+", "b-")
-    arrive(1, 0, 1, "a-", "b+", "b-")
+    arrive(-1, 0, 1, "b+", "b-")
+    arrive(1, 0, 0, "b+", "b-")
     arrive(0, -1, 0, "b+")
     arrive(0, 1, 1, "b-")
-
     z_arrive(2, 2, 0, 4)
     z_relay(3, 2, 0, 4, up)
     z_arrive(5, 6, 0, 4)
     z_relay(6, 6, 0, 4, down)
-    small_arrive(3, 12, 4)
-    small_push(5, "b+", 12, 8, 4)
-    small_arrive(4, 4, 4)
-
-    arrive(-1, 0, 1, "b+", "b-")
-    arrive(1, 0, 0, "b+", "b-")
-    arrive(0, -1, 1)
-    arrive(0, 1, 0)
-    z_arrive(3, 3, 0, 4)
-    z_half_up = z_block(bi, (z + DEPTH - 3) % DEPTH * 4, 2)
-    go(remote(z_half_up, z_half_up, z_send.at[4], z_recv.at[1], up))
-    z_arrive(6, 5, 0, 4)
-    z_half_down = z_block(bi, (z + DEPTH - 5) % DEPTH * 4 + 2, 2)
-    go(remote(z_half_down, z_half_down, z_send.at[7], z_recv.at[7], down))
-    multiply([(-1, 0), (1, 0)], "add")
     small_arrive(5, 8, 4)
     go(remote(fit.at[0], fit.at[1], s_send.at[12], s_recv.at[12], sibling))
-    multiply([(0, -1), (0, 1)], "add")
+    multiply([(-1, 0), (1, 0)], "add")
     arrive(2, 0, 0, "b+", "b-")
     arrive(2, 0, 1, "b+", "b-")
-    arrive(-1, -1, 0, "b+")
-    arrive(-1, 1, 0)
 
     remote(fit.at[0], fit.at[1], s_send.at[12], s_recv.at[12], sibling).wait_recv()
     wide = lax.broadcasted_iota(jnp.int32, (16, 128), 1)
@@ -307,8 +297,8 @@
         weights[0, first : first + 8] = coarse
         weights[1, first : first + 8] = both - coarse
 
-    arrive(1, -1, 1)
-    arrive(1, 1, 1, "b-")
+    arrive(0, -1, 1)
+    arrive(0, 1, 0)
 
     levels = lax.broadcasted_iota(jnp.int32, (128, 128), 0)
 
@@ -334,17 +324,20 @@
             coup[...] += nt(lhs, jnp.concatenate(hot(paired(past[0, r, 0])), axis=1))
 
     couple(0, 8)
-    arrive(0, 2, 0)
-    arrive(0, 2, 1)
+    arrive(-1, -1, 0, "b+")
+    arrive(-1, 1, 0)
+    z_arrive(3, 3, 0, 4)
+    z_half_up = z_block(bi, (z + DEPTH - 3) % DEPTH * 4, 2)
+    go(remote(z_half_up, z_half_up, z_send.at[4], z_recv.at[1], up))
+    z_arrive(6, 5, 0, 4)
+    z_half_down = z_block(bi, (z + DEPTH - 5) % DEPTH * 4 + 2, 2)
+    go(remote(z_half_down, z_half_down, z_send.at[7], z_recv.at[7], down))
     couple(8, 16)
     shares[0] = coup[:128, :] + coup[128:, :]
-    arrive(-1, -1, 1)
-    arrive(-1, 1, 1, "b-")
-    multiply([(2, 0), (0, 2)], "add")
+    multiply([(0, -1), (0, 1)], "add")
     go(remote(shares.at[0], shares.at[1], s_send.at[13], s_recv.at[13], sibling))
-    arrive(1, -1, 0, "b+")
-    arrive(1, 1, 0)
-    multiply([(-1, -1), (-1, 1)], "add")
+    arrive(1, -1, 1)
+    arrive(1, 1, 1, "b-")
     z_arrive(1, 4, 0, 2)
     z_arrive(7, 4, 2, 2)
 
@@ -361,10 +354,8 @@
     tokens = tok.shape[1]
     projected = lax.fori_loop(0, 2 * RING, project, jnp.zeros((tokens, 128), F32))
     p_high, p_low = halves(projected)
-    arrive(2, -1, 0, "b+")
-    arrive(2, 1, 0)
-    multiply([(1, -1), (1, 1)], "add")
-
+    arrive(-1, -1, 1)
+    arrive(-1, 1, 1, "b-")
     remote(shares.at[0], shares.at[1], s_send.at[13], s_recv.at[13], sibling).wait_recv()
     coupling = ((shares[0] + shares[1]) * (STEP_SCALE / (2.0 * (16 * 96 - 1)))).T
     c_high, c_low = halves(coupling)
@@ -372,9 +363,12 @@
     m_high, m_low = halves(nt(c_high, own_in) + nt(c_low, own_in))
     update = nn(jnp.concatenate([bo[...], bo[...]], axis=1), jnp.concatenate([m_high, m_low], axis=0))
     nw[...] = (w[0].astype(F32) + update).astype(BF16)
-    arrive(2, -1, 1)
-    arrive(2, 1, 1, "b-")
-
+    arrive(1, -1, 0, "b+")
+    arrive(1, 1, 0)
+    multiply([(-1, -1), (-1, 1)], "add")
+    arrive(0, 2, 0)
+    arrive(0, 2, 1)
+    multiply([(1, -1), (1, 1)], "add")
     outs, ins = hot(paired(seeds[0])), jnp.concatenate(hot(paired(seeds[1])), axis=1)
     picked = nn(jnp.concatenate([p_high, p_low], axis=1), jnp.concatenate([ins, ins], axis=0))
     member = lax.shift_right_logical(lax.broadcasted_iota(jnp.int32, picked.shape, 0), 4)
@@ -387,7 +381,12 @@
     z_high, z_low = halves(term)
     zz[0] = z_high
     zz[1] = z_low
-    multiply([(2, -1), (2, 1)], "term")
+    arrive(2, -1, 0, "b+")
+    arrive(2, 1, 0)
+    multiply([(2, 0), (0, 2)], "term")
+    arrive(2, -1, 1)
+    arrive(2, 1, 1, "b-")
+    multiply([(2, -1), (2, 1)], "add")
     arrive(-1, 2, 0)
     arrive(-1, 2, 1)
     arrive(1, 2, 0)
@@ -399,6 +398,18 @@
 
     for copy in pending:
         copy.wait_send()
+
+
+def finish(out, nw, hidden_hbm, nw_hbm, done):
+    third = out.shape[0] // 3
+    copies = [pltpu.make_async_copy(nw, nw_hbm, done.at[3])]
+    for k in range(3):
+        span = pl.ds(k * third, third)
+        copies.append(pltpu.make_async_copy(out.at[span], hidden_hbm.at[span], done.at[k]))
+    for copy in copies:
+        copy.start()
+    for copy in copies:
+        copy.wait()
 
 
 def shards(tokens, weight, bank_in, bank_out, fitness, past_seeds, new_seeds):
@@ -438,6 +449,17 @@
         tokens.reshape(flat, features), weight, bank_in.reshape(4, 128, 128), bank_out,
         fitness.reshape(1, members), past_seeds.transpose(1, 2, 0), new_seeds.transpose(1, 2, 0),
     )
+    hidden, new_weight = pl.pallas_call(
+        finish,
+        out_shape=(
+            jax.ShapeDtypeStruct((flat, rows), BF16),
+            jax.ShapeDtypeStruct((rows, wide), BF16),
+        ),
+        in_specs=[pl.BlockSpec(memory_space=pltpu.VMEM)] * 2,
+        out_specs=[pl.BlockSpec(memory_space=pl.ANY)] * 2,
+        scratch_shapes=[dma((4,))],
+        compiler_params=pltpu.CompilerParams(vmem_limit_bytes=32 * 1024 * 1024),
+    )(hidden, new_weight)
     return hidden.reshape(members, each, rows), new_weight
 
 

time: 68 us -> 63.1 us (0.928)
  Pallas kernels: 65 us -> 62.3 us
  local copies, waits for them, and re-layouts: 2.3 us -> 0 us
    pallas_call x1, Pallas kernels: 65 us -> 60.6 us  [shards(): pl.pallas_call(kernel, out_shape=(pltpu.VMEM((flat, rows), BF16), pltpu.V...]
    unnamed x2 -> x0, local copies, waits for them, and re-layouts: 2.3 us -> none
    pallas_call x0 -> x1, Pallas kernels: none -> 1.71 us  [shards(): pl.pallas_call(finish, out_shape=(jax.ShapeDtypeStruct((flat, rows), BF16...]
where the time goes in v3:
time: 63.1 us; the launch traced here: 63 us
  Pallas kernels  62.3 us (99%)
  between operations  0.64 us (1%)
    pallas_call x1, Pallas kernels, shards(): pl.pallas_call(kernel, out_shape=(pltpu.VMEM((flat, rows), BF16), pltpu.V...  60.6 us
    pallas_call x1, Pallas kernels, shards(): pl.pallas_call(finish, out_shape=(jax.ShapeDtypeStruct((flat, rows), BF16...  1.71 us

profile of v3, /device:TPU:1, one launch (start us, length us, event | category | flops | bytes accessed | tf_op | source)
XLA Modules:
  0.0 63.0 jit_solution(5879071151659355539)
XLA Ops:
  0.6 60.6 %shard_map.86 = (bf16[768,1792]{1,0:T(8,128)(2,1)S(1)}, bf16[1792,128]{1,0:T(8,128)(2,1)S(1)}) custom-call(bf16[768,4096]{1,0:T(8,128)(2,1)} %bitcast.6, bf16[1792,128]{1,0:T(8,128)(2,1)} %w_hbm.1, bf16[4,128,128]{2,1,0:T(8,128)(2,1)} %bitcast.7, bf16[1792,128]{1,0:T(8,128)(2,1)} %bo_hbm.1, s32[1,48]{1,0:T(1,128)} %bitcast.10, s32[2,8,48]{2,1,0:T(8,128)} %bitcast.8, ...), custom_call_target="tpu_custom_call" | custom-call | tf_op jit(solution)/shard_map/pallas_call | solution.py:421
  61.3 1.7 %shard_map.87 = (bf16[768,1792]{1,0:T(8,128)(2,1)}, bf16[1792,128]{1,0:T(8,128)(2,1)}) custom-call(bf16[768,1792]{1,0:T(8,128)(2,1)S(1)} %get-tuple-element.6.out, bf16[1792,128]{1,0:T(8,128)(2,1)S(1)} %get-tuple-element.7.nw), custom_call_target="tpu_custom_call" | custom-call | tf_op jit(solution)/shard_map/pallas_call | solution.py:452

commit v4 on v3

--- a/solution.py
+++ b/solution.py
@@ -38,13 +38,17 @@
     return (da % RING) * RING + db % RING
 
 
+LAST = (slot(2, 2), 16 + slot(2, 2))
+
+
 def one_hot_row(levels, row):
     return levels == jnp.broadcast_to(row, levels.shape)
 
 
 def kernel(
-    tok_hbm, w_hbm, bi_hbm, bo_hbm, fit_hbm, past_hbm, seeds_hbm, out, nw,
-    tok, w, bi, bo, past, fit, seeds, acc, weights, coup, shares, zz,
+    tok_hbm, w_hbm, bi_hbm, bo_hbm, fit_hbm, past_hbm, seeds_hbm,
+    acc, w_last, tok_last, nw,
+    tok, w, bi, bo, past, fit, seeds, weights, coup, shares, zz,
     send, recv, sib_send, sib_recv, z_send, z_recv, s_send, s_recv, tok_sem, local,
 ):
     x, y, c, z = (lax.axis_index(name) for name in (*POP, "row"))
@@ -88,7 +92,8 @@
         pending.append(copy)
 
     def part(index, h):
-        return w.at[index, pl.ds(h * half, half), :]
+        block = w_last.at[index // 16] if index in LAST else w.at[index]
+        return block.at[pl.ds(h * half, half), :]
 
     order = {name: place_at for place_at, name in enumerate(ways)}
 
@@ -172,11 +177,19 @@
                 loads[index] = pltpu.make_async_copy(
                     tok_hbm.at[:, pl.ds(start, 128)], tok.at[index], tok_sem.at[index]
                 )
+                if index in LAST:
+                    loads[32 + index // 16] = pltpu.make_async_copy(
+                        tok_hbm.at[:, pl.ds(start, 128)],
+                        tok_last.at[index // 16],
+                        tok_sem.at[32 + index // 16],
+                    )
     sequence = [(0, 0), (-1, 0), (1, 0), (0, -1), (0, 1), (2, 0), (0, 2), (-1, -1), (-1, 1),
                 (1, -1), (1, 1), (2, -1), (2, 1), (-1, 2), (1, 2), (2, 2)]
     for place_at in sequence:
         for at in (0, 16):
             loads[at + slot(*place_at)].start()
+    loads[32].start()
+    loads[33].start()
 
     def blocks_of(places):
         return [at + slot(*place_at) for place_at in places for at in (0, 16)]
@@ -194,19 +207,14 @@
             lhs += [zz[0], zz[1]]
         lhs = jnp.concatenate(lhs, axis=1)
 
-        @pl.loop(0, 2)
-        def _(h):
-            span = pl.ds(pl.multiple_of(h * half, half), half)
-            rhs = [w[block, span, :] for block in blocks]
-            if extra:
-                rhs += [bo[span, :], bo[span, :]]
-            product = nt(lhs, jnp.concatenate(rhs, axis=1))
-            if mode == "first":
-                acc[h] = product
-            elif mode == "last":
-                out[:, span] = (acc[h] + product).astype(BF16)
-            else:
-                acc[h] += product
+        rhs = [w[block] for block in blocks]
+        if extra:
+            rhs += [bo[...], bo[...]]
+        product = nt(lhs, jnp.concatenate(rhs, axis=1))
+        if mode == "first":
+            acc[...] = product
+        else:
+            acc[...] += product
 
     def z_arrive(k, behind, first, count):
         block = (z + DEPTH - behind) % DEPTH * 4 + first
@@ -353,7 +361,7 @@
 
     tokens = tok.shape[1]
     projected = lax.fori_loop(0, 2 * RING, project, jnp.zeros((tokens, 128), F32))
-    p_high, p_low = halves(projected)
+    p_high = projected.astype(BF16)
     arrive(-1, -1, 1)
     arrive(-1, 1, 1, "b-")
     remote(shares.at[0], shares.at[1], s_send.at[13], s_recv.at[13], sibling).wait_recv()
@@ -370,13 +378,12 @@
     arrive(0, 2, 1)
     multiply([(1, -1), (1, 1)], "add")
     outs, ins = hot(paired(seeds[0])), jnp.concatenate(hot(paired(seeds[1])), axis=1)
-    picked = nn(jnp.concatenate([p_high, p_low], axis=1), jnp.concatenate([ins, ins], axis=0))
+    picked = nn(p_high, ins)
     member = lax.shift_right_logical(lax.broadcasted_iota(jnp.int32, picked.shape, 0), 4)
     lane = lax.broadcasted_iota(jnp.int32, picked.shape, 1) & 63
-    g_high, g_low = halves(jnp.where(member == lane, picked * NOISE_SCALE, 0.0))
-    term = nt(
-        jnp.concatenate([p_high, p_low, p_high, g_high, g_low], axis=1),
-        jnp.concatenate([c_high, c_high, c_low, *outs, *outs], axis=1),
+    own_picks = jnp.where(member == lane, picked, 0.0).astype(BF16)
+    term = NOISE_SCALE * nt(own_picks, jnp.concatenate(outs, axis=1)) + nt(
+        jnp.concatenate([p_high, p_high], axis=1), jnp.concatenate([c_high, c_low], axis=1)
     )
     z_high, z_low = halves(term)
     zz[0] = z_high
@@ -394,22 +401,27 @@
     multiply([(-1, 2), (1, 2)], "add")
     arrive(2, 2, 0)
     arrive(2, 2, 1)
-    multiply([(2, 2)], "last")
+    sib_arrive(2, 2)
 
     for copy in pending:
         copy.wait_send()
 
 
-def finish(out, nw, hidden_hbm, nw_hbm, done):
-    third = out.shape[0] // 3
-    copies = [pltpu.make_async_copy(nw, nw_hbm, done.at[3])]
-    for k in range(3):
-        span = pl.ds(k * third, third)
-        copies.append(pltpu.make_async_copy(out.at[span], hidden_hbm.at[span], done.at[k]))
-    for copy in copies:
-        copy.start()
+def finish(acc, w_last, tok_last, nw, hidden_hbm, nw_hbm, out, done):
+    weights_out = pltpu.make_async_copy(nw, nw_hbm, done.at[2])
+    weights_out.start()
+    lhs = jnp.concatenate([tok_last[0], tok_last[1]], axis=1)
+    first = out.shape[1] * 4 // 7
+    copies = []
+    for k, (start, size) in enumerate(((0, first), (first, out.shape[1] - first))):
+        span = pl.ds(start, size)
+        rhs = jnp.concatenate([w_last[0, span, :], w_last[1, span, :]], axis=1)
+        out[:, span] = (acc[:, span] + nt(lhs, rhs)).astype(BF16)
+        copies.append(pltpu.make_async_copy(out.at[:, span], hidden_hbm.at[:, span], done.at[k]))
+        copies[-1].start()
     for copy in copies:
         copy.wait()
+    weights_out.wait()
 
 
 def shards(tokens, weight, bank_in, bank_out, fitness, past_seeds, new_seeds):
@@ -418,14 +430,16 @@
     flat = members * each
     seeds = (*past_seeds.shape[1:], members)
     dma = pltpu.SemaphoreType.DMA
-    hidden, new_weight = pl.pallas_call(
+    parts = pl.pallas_call(
         kernel,
         out_shape=(
-            pltpu.VMEM((flat, rows), BF16),
+            pltpu.VMEM((flat, rows), F32),
+            pltpu.VMEM((2, rows, 128), BF16),
+            pltpu.VMEM((2, flat, 128), BF16),
             pltpu.VMEM((rows, wide), BF16),
         ),
         in_specs=[pl.BlockSpec(memory_space=pl.ANY)] * 7,
-        out_specs=[pl.BlockSpec(memory_space=pltpu.VMEM)] * 2,
+        out_specs=[pl.BlockSpec(memory_space=pltpu.VMEM)] * 4,
         scratch_shapes=[
             pltpu.VMEM((32, flat, 128), BF16),
             pltpu.VMEM((32, rows, 128), BF16),
@@ -434,16 +448,15 @@
             pltpu.VMEM((2, 16, *seeds), jnp.int32),
             pltpu.VMEM((2, 16, 1, members), jnp.int32),
             pltpu.VMEM(seeds, jnp.int32),
-            pltpu.VMEM((2, flat, rows // 2), F32),
             pltpu.VMEM((2, 16, 128), F32),
             pltpu.VMEM((256, 128), F32),
             pltpu.VMEM((2, 128, 128), F32),
             pltpu.VMEM((2, flat, 128), BF16),
             dma((128,)), dma((32,)), dma((32,)), dma((32,)), dma((8,)), dma((8,)),
-            dma((14,)), dma((14,)), dma((32,)), dma((6,)),
+            dma((14,)), dma((14,)), dma((34,)), dma((6,)),
         ],
         compiler_params=pltpu.CompilerParams(
-            collective_id=0, has_side_effects=True, vmem_limit_bytes=56 * 1024 * 1024
+            collective_id=0, has_side_effects=True, vmem_limit_bytes=52 * 1024 * 1024
         ),
     )(
         tokens.reshape(flat, features), weight, bank_in.reshape(4, 128, 128), bank_out,
@@ -455,11 +468,11 @@
             jax.ShapeDtypeStruct((flat, rows), BF16),
             jax.ShapeDtypeStruct((rows, wide), BF16),
         ),
-        in_specs=[pl.BlockSpec(memory_space=pltpu.VMEM)] * 2,
+        in_specs=[pl.BlockSpec(memory_space=pltpu.VMEM)] * 4,
         out_specs=[pl.BlockSpec(memory_space=pl.ANY)] * 2,
-        scratch_shapes=[dma((4,))],
+        scratch_shapes=[pltpu.VMEM((flat, rows), BF16), dma((3,))],
         compiler_params=pltpu.CompilerParams(vmem_limit_bytes=32 * 1024 * 1024),
-    )(hidden, new_weight)
+    )(*parts)
     return hidden.reshape(members, each, rows), new_weight
 
 

time: 63.1 us -> 60.3 us (0.956)
  Pallas kernels: 62.3 us -> 59.4 us
    pallas_call x1, Pallas kernels: 60.6 us -> 57.1 us  [shards(): pl.pallas_call(kernel, out_shape=(pltpu.VMEM((flat, rows), F32), pltpu.VM...]
where the time goes in v4:
time: 60.3 us; the launch traced here: 60.2 us
  Pallas kernels  59.4 us (99%)
  between operations  0.8 us (1%)
    pallas_call x1, Pallas kernels, shards(): pl.pallas_call(kernel, out_shape=(pltpu.VMEM((flat, rows), F32), pltpu.VM...  57.1 us
    pallas_call x1, Pallas kernels, shards(): pl.pallas_call(finish, out_shape=(jax.ShapeDtypeStruct((flat, rows), BF16...  2.28 us

profile of v4, /device:TPU:1, one launch (start us, length us, event | category | flops | bytes accessed | tf_op | source)
XLA Modules:
  0.0 60.2 jit_solution(11911555341354248651)
XLA Ops:
  0.6 57.1 %shard_map.86 = (f32[768,1792]{1,0:T(8,128)S(1)}, bf16[2,1792,128]{2,1,0:T(8,128)(2,1)S(1)}, bf16[2,768,128]{2,1,0:T(8,128)(2,1)S(1)}, bf16[1792,128]{1,0:T(8,128)(2,1)S(1)}) custom-call(bf16[768,4096]{1,0:T(8,128)(2,1)} %bitcast.6, bf16[1792,128]{1,0:T(8,128)(2,1)} %w_hbm.1, bf16[4,128,128]{2,1,0:T(8,128)(2,1)} %bitcast.7, bf16[1792,128]{1,0:T(8,128)(2,1)} %bo_hbm.1, ...), custom_call_target="tpu_custom_call" | custom-call | tf_op jit(solution)/shard_map/pallas_call | solution.py:433
  57.8 2.3 %shard_map.87 = (bf16[768,1792]{1,0:T(8,128)(2,1)}, bf16[1792,128]{1,0:T(8,128)(2,1)}) custom-call(f32[768,1792]{1,0:T(8,128)S(1)} %get-tuple-element.8.acc, bf16[2,1792,128]{2,1,0:T(8,128)(2,1)S(1)} %get-tuple-element.9.w_last, bf16[2,768,128]{2,1,0:T(8,128)(2,1)S(1)} %get-tuple-element.10.tok_last, bf16[1792,128]{1,0:T(8,128)(2,1)S(1)} %get-tuple-element.11.nw), custom_call_target="tpu_custom_call" | custom-call | tf_op jit(solution)/shard_map/pallas_call | solution.py:465

commit v5 on v4

--- a/solution.py
+++ b/solution.py
@@ -390,17 +390,17 @@
     zz[1] = z_low
     arrive(2, -1, 0, "b+")
     arrive(2, 1, 0)
-    multiply([(2, 0), (0, 2)], "term")
     arrive(2, -1, 1)
     arrive(2, 1, 1, "b-")
-    multiply([(2, -1), (2, 1)], "add")
+    multiply([(2, 0), (0, 2)], "term")
     arrive(-1, 2, 0)
     arrive(-1, 2, 1)
+    multiply([(2, -1), (2, 1)], "add")
     arrive(1, 2, 0)
     arrive(1, 2, 1)
-    multiply([(-1, 2), (1, 2)], "add")
     arrive(2, 2, 0)
     arrive(2, 2, 1)
+    multiply([(-1, 2), (1, 2)], "add")
     sib_arrive(2, 2)
 
     for copy in pending:

time: 60.3 us -> 57.2 us (0.949)
  Pallas kernels: 59.4 us -> 56.3 us
    pallas_call x1, Pallas kernels: 57.1 us -> 54.1 us  [shards(): pl.pallas_call(kernel, out_shape=(pltpu.VMEM((flat, rows), F32), pltpu.VM...]
where the time goes in v5:
time: 57.2 us; the launch traced here: 57.1 us
  Pallas kernels  56.3 us (98%)
  between operations  0.8 us (1%)
    pallas_call x1, Pallas kernels, shards(): pl.pallas_call(kernel, out_shape=(pltpu.VMEM((flat, rows), F32), pltpu.VM...  54.1 us
    pallas_call x1, Pallas kernels, shards(): pl.pallas_call(finish, out_shape=(jax.ShapeDtypeStruct((flat, rows), BF16...  2.27 us

profile of v5, /device:TPU:1, one launch (start us, length us, event | category | flops | bytes accessed | tf_op | source)
XLA Modules:
  0.0 57.1 jit_solution(10544844891474639760)
XLA Ops:
  0.6 54.1 %shard_map.86 = (f32[768,1792]{1,0:T(8,128)S(1)}, bf16[2,1792,128]{2,1,0:T(8,128)(2,1)S(1)}, bf16[2,768,128]{2,1,0:T(8,128)(2,1)S(1)}, bf16[1792,128]{1,0:T(8,128)(2,1)S(1)}) custom-call(bf16[768,4096]{1,0:T(8,128)(2,1)} %bitcast.6, bf16[1792,128]{1,0:T(8,128)(2,1)} %w_hbm.1, bf16[4,128,128]{2,1,0:T(8,128)(2,1)} %bitcast.7, bf16[1792,128]{1,0:T(8,128)(2,1)} %bo_hbm.1, ...), custom_call_target="tpu_custom_call" | custom-call | tf_op jit(solution)/shard_map/pallas_call | solution.py:433
  54.7 2.3 %shard_map.87 = (bf16[768,1792]{1,0:T(8,128)(2,1)}, bf16[1792,128]{1,0:T(8,128)(2,1)}) custom-call(f32[768,1792]{1,0:T(8,128)S(1)} %get-tuple-element.8.acc, bf16[2,1792,128]{2,1,0:T(8,128)(2,1)S(1)} %get-tuple-element.9.w_last, bf16[2,768,128]{2,1,0:T(8,128)(2,1)S(1)} %get-tuple-element.10.tok_last, bf16[1792,128]{1,0:T(8,128)(2,1)S(1)} %get-tuple-element.11.nw), custom_call_target="tpu_custom_call" | custom-call | tf_op jit(solution)/shard_map/pallas_call | solution.py:465

commit v6 on v5

--- a/solution.py
+++ b/solution.py
@@ -395,9 +395,9 @@
     multiply([(2, 0), (0, 2)], "term")
     arrive(-1, 2, 0)
     arrive(-1, 2, 1)
-    multiply([(2, -1), (2, 1)], "add")
     arrive(1, 2, 0)
     arrive(1, 2, 1)
+    multiply([(2, -1), (2, 1)], "add")
     arrive(2, 2, 0)
     arrive(2, 2, 1)
     multiply([(-1, 2), (1, 2)], "add")
@@ -408,13 +408,13 @@
 
 
 def finish(acc, w_last, tok_last, nw, hidden_hbm, nw_hbm, out, done):
-    weights_out = pltpu.make_async_copy(nw, nw_hbm, done.at[2])
+    weights_out = pltpu.make_async_copy(nw, nw_hbm, done.at[4])
     weights_out.start()
     lhs = jnp.concatenate([tok_last[0], tok_last[1]], axis=1)
-    first = out.shape[1] * 4 // 7
+    wide = out.shape[1]
     copies = []
-    for k, (start, size) in enumerate(((0, first), (first, out.shape[1] - first))):
-        span = pl.ds(start, size)
+    for k, start in enumerate(range(0, wide, 512)):
+        span = pl.ds(start, min(512, wide - start))
         rhs = jnp.concatenate([w_last[0, span, :], w_last[1, span, :]], axis=1)
         out[:, span] = (acc[:, span] + nt(lhs, rhs)).astype(BF16)
         copies.append(pltpu.make_async_copy(out.at[:, span], hidden_hbm.at[:, span], done.at[k]))
@@ -470,7 +470,7 @@
         ),
         in_specs=[pl.BlockSpec(memory_space=pltpu.VMEM)] * 4,
         out_specs=[pl.BlockSpec(memory_space=pl.ANY)] * 2,
-        scratch_shapes=[pltpu.VMEM((flat, rows), BF16), dma((3,))],
+        scratch_shapes=[pltpu.VMEM((flat, rows), BF16), dma((5,))],
         compiler_params=pltpu.CompilerParams(vmem_limit_bytes=32 * 1024 * 1024),
     )(*parts)
     return hidden.reshape(members, each, rows), new_weight

time: 57.2 us -> 57 us (level)
  no operation moved by 1% of the time
where the time goes in v6:
time: 57 us; the launch traced here: 56.9 us
  Pallas kernels  56.1 us (98%)
  between operations  0.8 us (1%)
    pallas_call x1, Pallas kernels, shards(): pl.pallas_call(kernel, out_shape=(pltpu.VMEM((flat, rows), F32), pltpu.VM...  54 us
    pallas_call x1, Pallas kernels, shards(): pl.pallas_call(finish, out_shape=(jax.ShapeDtypeStruct((flat, rows), BF16...  2.09 us

profile of v6, /device:TPU:1, one launch (start us, length us, event | category | flops | bytes accessed | tf_op | source)
XLA Modules:
  0.0 56.9 jit_solution(16862677235760643760)
XLA Ops:
  0.6 54.0 %shard_map.86 = (f32[768,1792]{1,0:T(8,128)S(1)}, bf16[2,1792,128]{2,1,0:T(8,128)(2,1)S(1)}, bf16[2,768,128]{2,1,0:T(8,128)(2,1)S(1)}, bf16[1792,128]{1,0:T(8,128)(2,1)S(1)}) custom-call(bf16[768,4096]{1,0:T(8,128)(2,1)} %bitcast.6, bf16[1792,128]{1,0:T(8,128)(2,1)} %w_hbm.1, bf16[4,128,128]{2,1,0:T(8,128)(2,1)} %bitcast.7, bf16[1792,128]{1,0:T(8,128)(2,1)} %bo_hbm.1, ...), custom_call_target="tpu_custom_call" | custom-call | tf_op jit(solution)/shard_map/pallas_call | solution.py:433
  54.7 2.1 %shard_map.87 = (bf16[768,1792]{1,0:T(8,128)(2,1)}, bf16[1792,128]{1,0:T(8,128)(2,1)}) custom-call(f32[768,1792]{1,0:T(8,128)S(1)} %get-tuple-element.8.acc, bf16[2,1792,128]{2,1,0:T(8,128)(2,1)S(1)} %get-tuple-element.9.w_last, bf16[2,768,128]{2,1,0:T(8,128)(2,1)S(1)} %get-tuple-element.10.tok_last, bf16[1792,128]{1,0:T(8,128)(2,1)S(1)} %get-tuple-element.11.nw), custom_call_target="tpu_custom_call" | custom-call | tf_op jit(solution)/shard_map/pallas_call | solution.py:465
